TPU v7x, 512 devices: a whole 4x4x16 slice. The times are simulated.
512 devices in a mesh: ctx: 64 (over y_hi, z, core), head: 8 (over x, y_lo).
Axes of the slice: x: 4, y: 4 (y_hi: 2, y_lo: 2; y = y_hi * 2 + y_lo), z: 16, core: 2. Of those that a mesh axis runs over, the one named last changes fastest.
Arguments:
- clean_latents: bfloat16 [128, 4, 8, 128], P('ctx'), may hold values from -6 to 6
- noise: bfloat16 [128, 4, 8, 128], P('ctx'), may hold values from -6 to 6
- timesteps: int32 [128], P('ctx'), may hold values from 0 to 999
- span_order: int32 [128], P('ctx'), may hold values from 0 to 127, as said below
- valid_frames: int32 [128], P('ctx'), may hold values from 1 to 4
- embed_weight: bfloat16 [256, 6144], P(None, 'head'), may hold values from -0.375 to 0.375
- position: bfloat16 [8192, 6144], P('ctx'), may hold values from -6 to 6
- norm_gain: bfloat16 [6144], replicated, may hold values from 0.099609375 to 1.8984375
- query_weight: bfloat16 [6144, 3072], P('ctx', 'head'), as said below
- kv_weight: bfloat16 [6144, 2048], P('ctx', 'head'), as said below
Outputs:
- attended: bfloat16 [8192, 3072], P('ctx', 'head')
Inputs may be any that keep to these rules, and one draw needn't show every extreme that they name: `span_order`: span slots 2d and 2d + 1 hold spans p and 127 - p for some p, in either order; each span number stands once. `query_weight`: entries scale with the fan-in 6144. `kv_weight`: entries scale with the fan-in 6144.
All inputs are finite; a program needn't handle non-finite values.
Results may differ from a plain program's by a relative error of at most 0.012.
The roundings to bfloat16 on the way count: a program that leaves them out, or rounds other values in their place, can miss the bound.
Values may be sent and summed in bfloat16 or wider, within the bound.
No kernel may reach another device: no remote copies, remote signals or barrier semaphores. Data moves between devices by JAX's collectives and lax.ppermute only.
A program may use at most 64 MiB of HBM per device.

v0:
```python
import math
import jax
import jax.numpy as jnp
from jax import lax
from jax.sharding import PartitionSpec as P

HD = 128
CH = 16
eps_norm = 1e-06
masked_low = -1e30


def make_patches(latents):
    slots, frames, height, flat = latents.shape
    width = flat // CH
    grid = latents.reshape(slots, frames, height, width, CH)
    padded = jnp.pad(grid, ((0, 0), (0, 0), (1, 1), (1, 1), (0, 0)))
    half_rows = height // 2
    half_cols = width // 2
    split = padded.reshape(slots, frames, half_rows + 1, 2, half_cols + 1, 2, CH)
    offsets_list = []
    for row_off in range(4):
        for col_off in range(4):
            offsets_list.append(
                split[
                    :,
                    :,
                    row_off // 2 : row_off // 2 + half_rows,
                    row_off % 2,
                    col_off // 2 : col_off // 2 + half_cols,
                    col_off % 2,
                    :,
                ]
            )
    stacked = jnp.stack(offsets_list, axis=4)
    return stacked.reshape(slots * frames * half_rows * half_cols, 16 * CH)


def rms_normalize(values, gain):
    wide = values.astype(jnp.float32)
    factor = lax.rsqrt(jnp.mean(wide * wide, axis=-1, keepdims=True) + eps_norm)
    return (wide * factor * gain.astype(jnp.float32)).astype(jnp.bfloat16)


def attend(carry, query_heads, kv_block, allowed):
    largest, total, summed = carry
    local_heads = query_heads.shape[1]
    blocks = kv_block.reshape(kv_block.shape[0], local_heads, 2, HD)
    scores = jnp.einsum(
        "tkgd,nkd->tkgn", query_heads, blocks[:, :, 0], preferred_element_type=jnp.float32
    ) * HD ** (-0.5)
    mask = allowed[:, None, None, :]
    lowered = jnp.where(mask, scores, masked_low)
    new_largest = jnp.maximum(largest, jnp.max(lowered, axis=-1))
    raw = jnp.where(mask, jnp.exp(lowered - new_largest[..., None]), 0.0)
    factor = jnp.exp(largest - new_largest)
    total = total * factor + jnp.sum(raw, axis=-1)
    summed = summed * factor[..., None] + jnp.einsum(
        "tkgn,nkd->tkgd",
        raw.astype(jnp.bfloat16),
        blocks[:, :, 1],
        preferred_element_type=jnp.float32,
    )
    return (new_largest, total, summed)


def expand_rows(values, span_rows):
    return (values[:, None] + jnp.zeros((1, span_rows), jnp.int32)).reshape(
        values.shape[0] * span_rows
    )


def add_position(projected, position_rows, tokens):
    cols = projected.shape[1]
    doubled = projected.reshape(2, tokens, cols) + position_rows.astype(jnp.float32)[None]
    return doubled.reshape(2 * tokens, cols).astype(jnp.bfloat16)


def on_device(
    clean_latents,
    noise,
    timesteps,
    span_order,
    valid_frames,
    embed_weight,
    position,
    norm_gain,
    query_weight,
    kv_weight,
):
    slots = clean_latents.shape[0]
    frames = clean_latents.shape[1]
    frame_rows = clean_latents.shape[2] // 2 * (clean_latents.shape[3] // (2 * CH))
    span_rows = frames * frame_rows
    tokens = slots * span_rows
    level = ((timesteps.astype(jnp.float32) + 1.0) / 1000.0)[:, None, None, None]
    noisy_latents = (
        (1.0 - level) * clean_latents.astype(jnp.float32) + level * noise.astype(jnp.float32)
    ).astype(jnp.bfloat16)
    patches = jnp.concatenate([make_patches(noisy_latents), make_patches(clean_latents)], axis=0)
    col_count = embed_weight.shape[1]
    col_start = lax.axis_index("head") * col_count
    position_cols = lax.dynamic_slice_in_dim(position, col_start, col_count, 1)
    projected = jnp.dot(patches, embed_weight, preferred_element_type=jnp.float32)
    partial_cols = add_position(projected, position_cols, tokens)
    embedded = lax.all_gather(partial_cols, "head", axis=1, tiled=True)
    normed = rms_normalize(embedded, norm_gain)
    normed_noisy = normed[:tokens]
    query_cols = query_weight.shape[1]
    kv_cols = kv_weight.shape[1]
    local_heads = kv_cols // (2 * HD)
    group_size = query_cols // (local_heads * HD)
    row_ids = jnp.arange(tokens, dtype=jnp.int32)
    query_slot = row_ids // span_rows
    query_frame = row_ids % span_rows // frame_rows
    query_span = expand_rows(span_order, span_rows)
    query_valid = expand_rows(valid_frames, span_rows)
    query_live = query_frame < query_valid

    def fold_block(carry, query_heads, kv_piece, order_piece, valid_piece):
        rows = kv_piece.shape[0]
        key_span = expand_rows(order_piece, span_rows)
        key_valid = expand_rows(valid_piece, span_rows)
        key_frame = jnp.arange(rows, dtype=jnp.int32) % span_rows // frame_rows
        allowed = (key_span[None, :] < query_span[:, None]) & (key_frame < key_valid)[None, :]
        return attend(carry, query_heads, kv_piece, allowed)

    start_carry = (
        jnp.full((tokens, local_heads, group_size), masked_low, jnp.float32),
        jnp.zeros((tokens, local_heads, group_size), jnp.float32),
        jnp.zeros((tokens, local_heads, group_size, HD), jnp.float32),
    )
    own_allowed = (query_slot[:, None] == query_slot[None, :]) & query_live[None, :]
    columns = normed_noisy
    query_sum = jnp.dot(
        columns,
        lax.all_gather(query_weight, "ctx", axis=0, tiled=True),
        preferred_element_type=jnp.float32,
    )
    columns = normed
    kv_sum = jnp.dot(
        columns,
        lax.all_gather(kv_weight, "ctx", axis=0, tiled=True),
        preferred_element_type=jnp.float32,
    )
    query_heads = query_sum.astype(jnp.bfloat16).reshape(tokens, local_heads, group_size, HD)
    keys_values = kv_sum.astype(jnp.bfloat16)
    carry = attend(start_carry, query_heads, keys_values[:tokens], own_allowed)
    piece = (
        lax.all_gather(keys_values[tokens:], "ctx", axis=0, tiled=True),
        lax.all_gather(span_order, "ctx", axis=0, tiled=True),
        lax.all_gather(valid_frames, "ctx", axis=0, tiled=True),
    )
    kv_all = piece[0]
    order_all = piece[1]
    valid_all = piece[2]
    all_spans = order_all.shape[0]
    block_spans = math.gcd(all_spans, max(1, 1024 // span_rows))
    block_count = all_spans // block_spans
    kv_blocks = kv_all.reshape(block_count, block_spans * span_rows, kv_cols)
    order_blocks = order_all.reshape(block_count, block_spans)
    valid_blocks = valid_all.reshape(block_count, block_spans)

    def scan_step(state, piece):
        return (fold_block(state, query_heads, piece[0], piece[1], piece[2]), None)

    result, unused = lax.scan(scan_step, carry, (kv_blocks, order_blocks, valid_blocks))
    carry = result
    largest, total, summed = carry
    result = summed / total[..., None]
    result = jnp.where(query_live[:, None, None, None], result, 0.0)
    return result.reshape(tokens, query_cols).astype(jnp.bfloat16)


def solution(mesh):
    return jax.shard_map(
        on_device,
        mesh=mesh,
        in_specs=(
            P("ctx", None, None, None),
            P("ctx", None, None, None),
            P("ctx"),
            P("ctx"),
            P("ctx"),
            P(None, "head"),
            P("ctx", None),
            P(),
            P("ctx", "head"),
            P("ctx", "head"),
        ),
        out_specs=P("ctx", "head"),
        check_vma=False,
    )
```

profile of v0, /device:TPU:1, one launch (start us, length us, event | category | flops | bytes accessed | tf_op | source)
XLA Modules:
  0.0 587.3 jit_solution(14975481105577285705)
XLA Ops:
  6.6 0.9 reshape.412
  8.1 0.3 copy.86
  8.4 0.5 reshape.414
  9.8 0.3 copy.68
  10.1 0.5 reshape.411
  10.6 1.0 dynamic-slice_convert_fusion
  11.6 1.0 fusion.27
  12.7 0.7 all-gather.7.cloned.1.call-update
  13.5 0.7 all-gather.9.cloned.1.call-update
  14.2 0.6 convert_element_type.58
  14.8 81.0 %all-gather.5.cloned.1.call-done = bf16[256,6144]{1,0:T(8,128)(2,1)} async-done(((bf16[256,768]{1,0:T(8,128)(2,1)}), bf16[256,6144]{1,0:T(8,128)(2,1)}) %all-gather.5.cloned.1.call-update) | async-done | bytes 3145744 | tf_op jit(solution)/shard_map/all_gather | solution.py:106
  95.8 2.7 fusion.22
  98.7 1.8 fusion.24
  100.5 148.0 %all-gather.7.cloned.1.call-done = bf16[6144,256]{1,0:T(8,128)(2,1)} async-done(((bf16[96,256]{1,0:T(8,128)(2,1)}), bf16[6144,256]{1,0:T(8,128)(2,1)}) %all-gather.7.cloned.1.call-update) | async-done | bytes 3145744 | tf_op jit(solution)/shard_map/all_gather | solution.py:143
  248.5 3.2 convolution_convert_fusion
  251.7 0.7 fusion.50
  252.6 1.3 dynamic-slice
  254.5 0.5 jit_remainder_.8.clone.1
  255.0 1.3 dynamic-update-slice.1
  256.5 17.4 %all-reduce.4 = (s32[128]{0:T(128)S(1)}, s32[128]{0:T(128)S(1)}) all-reduce(s32[128]{0:T(128)S(1)} %dynamic-update-slice, s32[128]{0:T(128)} %dynamic-update-slice.1), channel_id=1, replica_groups=mesh['ctx'=64,'head'=8] {'ctx'}, use_global_device_ids=true, to_apply=%add.2 | all-reduce | flops 256 | bytes 2048
  273.9 0.7 reshape.420
  274.6 0.7 reshape.421
  275.3 0.5 copy-done.5
  275.9 123.5 %all-gather.9.cloned.1.call-done = bf16[6144,384]{1,0:T(8,128)(2,1)} async-done(((bf16[96,384]{1,0:T(8,128)(2,1)}), bf16[6144,384]{1,0:T(8,128)(2,1)}) %all-gather.9.cloned.1.call-update) | async-done | bytes 4718608 | tf_op jit(solution)/shard_map/all_gather | solution.py:137
  399.4 4.0 fusion.31
  403.4 1.0 copy.88
  404.5 1.0 fusion.51
  405.6 0.9 fusion.30
  406.5 138.1 %all-gather.11.cloned.1.call-done = bf16[8192,256]{0,1:T(8,128)(2,1)} async-done(((bf16[128,256]{0,1:T(8,128)(2,1)}), bf16[8192,256]{0,1:T(8,128)(2,1)}) %all-gather.11.cloned.1.call-update) | async-done | bytes 4194320 | tf_op jit(solution)/shard_map/all_gather | solution.py:150
  544.6 4.8 copy.132
  549.4 30.5 %while.17 = (s32[]{:T(128)}, f32[128,1,3]{0,2,1:T(4,128)S(1)}, f32[128,1,3]{0,2,1:T(4,128)S(1)}, f32[128,1,3,128]{0,3,2,1:T(8,128)S(1)}, s32[8,16]{1,0:T(8,128)}...) while((s32[]{:T(128)}, f32[128,1,3]{0,2,1:T(4,128)S(1)}, ...), condition=%wide.region_6.7_spmd.clone, body=%wide.region_3.6_spmd.clone.sunk | while | flops 205249664 | bytes 7370237 | solution.py:167
  549.4 1.1 constant_dynamic-slice_fusion.4
  550.6 0.7 fusion.65
  551.9 0.4 fusion.67
  552.7 0.4 fusion.70
  553.2 1.1 constant_dynamic-slice_fusion.4
  554.4 0.7 fusion.65
  555.8 0.4 fusion.67
  556.5 0.4 fusion.70
  557.0 1.1 constant_dynamic-slice_fusion.4
  558.2 0.7 fusion.65
  559.6 0.4 fusion.67
  560.4 0.4 fusion.70
  560.8 1.1 constant_dynamic-slice_fusion.4
  562.1 0.7 fusion.65
  563.4 0.4 fusion.67
  564.2 0.4 fusion.70
  564.6 1.1 constant_dynamic-slice_fusion.4
  565.9 0.7 fusion.65
  567.2 0.4 fusion.67
  568.0 0.4 fusion.70
  568.5 1.1 constant_dynamic-slice_fusion.4
  569.7 0.7 fusion.65
  571.0 0.4 fusion.67
  571.8 0.4 fusion.70
  572.3 1.1 constant_dynamic-slice_fusion.4
  573.5 0.7 fusion.65
  574.9 0.4 fusion.67
  575.7 0.4 fusion.70
  576.1 1.1 constant_dynamic-slice_fusion.4
  577.3 0.7 fusion.65
  578.7 0.4 fusion.67
  579.5 0.4 fusion.70
  580.0 0.8 copy.94
  (176 shorter events, 11.4 us)
Async XLA Ops:
  6.5 5.1 copy-start
  6.5 2.4 copy-start.2
  6.5 2.4 copy-start.7
  6.5 2.4 copy-start.3
  6.5 89.3 %all-gather.5.cloned.1.call-start = ((), (), s32[]{:S(2)}) async-start(), calls=%async_computation | async-start | bytes 3538944 | tf_op jit(solution)/shard_map/all_gather | solution.py:106
  9.5 4.7 copy-start.4
  12.7 235.8 %all-gather.7.cloned.1.call-start = ((), (), s32[]{:S(2)}) async-start(), calls=%async_computation.1 | async-start | bytes 3194880 | tf_op jit(solution)/shard_map/all_gather | solution.py:143
  13.4 386.0 %all-gather.9.cloned.1.call-start = ((), (), s32[]{:S(2)}) async-start(), calls=%async_computation.2 | async-start | bytes 4792320 | tf_op jit(solution)/shard_map/all_gather | solution.py:137
  14.2 530.4 %all-gather.11.cloned.1.call-start = ((), (), s32[]{:S(2)}) async-start(), calls=%async_computation.3 | async-start | bytes 4259840 | tf_op jit(solution)/shard_map/all_gather | solution.py:150
  95.8 2.8 copy-start.1
  100.5 151.9 %copy-start.8 = (s32[2]{0:T(128)S(1)}, s32[2]{0:T(128)}, u32[]{:S(2)}) copy-start(s32[2]{0:T(128)} %param.16) | copy-start | bytes 28
  100.5 155.8 %copy-start.9 = (s32[2]{0:T(128)S(1)}, s32[2]{0:T(128)}, u32[]{:S(2)}) copy-start(s32[2]{0:T(128)} %param.15) | copy-start | bytes 28
  275.3 0.5 copy-start.5
  544.6 4.8 copy-start.10
  549.4 30.6 %copy-start.6 = (pred[128]{0:T(512)(128)(4,1)S(1)}, pred[128]{0:T(512)(128)(4,1)}, u32[]{:S(2)}) copy-start(pred[128]{0:T(512)(128)(4,1)} %copy-done.5) | copy-start | bytes 388
Sparse Core Ops, SparseCore 0:
  12.8 82.9 all-gather.4
  99.1 149.3 all-gather.6
  251.8 147.5 all-gather.8
  402.2 142.2 all-gather.10
where the time goes:
time: 588 us; the launch traced here: 587 us
  waiting for transfers between devices  492 us (84%)
  local copies, waits for them, and re-layouts  34.2 us (6%)
  blocking collectives  17.4 us (3%)
  matrix products  17.1 us (3%)
  between operations  14.2 us (2%)
  other arithmetic  11.9 us (2%)
    all_gather x1, waiting for transfers between devices, on_device(): lax.all_gather(kv_weight, 'ctx', axis=0, tiled=True)  148 us
    all_gather x1, waiting for transfers between devices, on_device(): lax.all_gather(keys_values[tokens:], 'ctx', axis=0, tiled=True)  138 us
    all_gather x1, waiting for transfers between devices, on_device(): lax.all_gather(query_weight, 'ctx', axis=0, tiled=True)  123 us
    all_gather x1, waiting for transfers between devices, on_device(): embedded = lax.all_gather(partial_cols, 'head', axis=1, tiled=True)  81 us
    unnamed x1, blocking collectives  17.4 us
  transfers between devices with their start and end apart: 4, of which 4 were waited for; matrix products, arithmetic and copies ran while one was open for 4% of the time, Pallas kernels for 0%

commit v1 on v0

--- a/solution.py
+++ b/solution.py
@@ -134,7 +134,9 @@
     columns = normed_noisy
     query_sum = jnp.dot(
         columns,
-        lax.all_gather(query_weight, "ctx", axis=0, tiled=True),
+        jnp.concatenate(
+            lax.all_to_all(jnp.stack([query_weight] * lax.axis_size("ctx")), "ctx", 0, 0), axis=0
+        ),
         preferred_element_type=jnp.float32,
     )
     columns = normed

time: 588 us -> 505 us (0.86)
  waiting for transfers between devices: 492 us -> 380 us
  starting transfers between devices: 0.15 us -> 20.2 us
  local copies, waits for them, and re-layouts: 34.2 us -> 42 us
    all_gather x1 -> x0, waiting for transfers between devices: 123 us -> none  [on_device(): lax.all_gather(query_weight, 'ctx', axis=0, tiled=True)]
    all_gather x1, waiting for transfers between devices: 148 us -> 185 us  [on_device(): lax.all_gather(kv_weight, 'ctx', axis=0, tiled=True)]
    all_gather x1, waiting for transfers between devices: 138 us -> 118 us  [on_device(): lax.all_gather(keys_values[tokens:], 'ctx', axis=0, tiled=True)]
    all_to_all x0 -> x1, starting transfers between devices: none -> 20.1 us  [on_device(): lax.all_to_all(jnp.stack([query_weight] * lax.axis_size('ctx')), 'ctx', 0...]
  transfers between devices with their start and end apart: 4 -> 4, of which waited for: 4 -> 3; matrix products, arithmetic and copies ran while one was open for 4% -> 4% of each run, Pallas kernels for 0% -> 0%
where the time goes in v1:
time: 505 us; the launch traced here: 504 us
  waiting for transfers between devices  380 us (75%)
  local copies, waits for them, and re-layouts  42 us (8%)
  starting transfers between devices  20.2 us (4%)
  blocking collectives  18.1 us (4%)
  matrix products  17.1 us (3%)
  between operations  14.2 us (3%)
  other arithmetic  11.9 us (2%)
    all_gather x1, waiting for transfers between devices, on_device(): lax.all_gather(kv_weight, 'ctx', axis=0, tiled=True)  185 us
    all_gather x1, waiting for transfers between devices, on_device(): lax.all_gather(keys_values[tokens:], 'ctx', axis=0, tiled=True)  118 us
    all_gather x1, waiting for transfers between devices, on_device(): embedded = lax.all_gather(partial_cols, 'head', axis=1, tiled=True)  76.2 us
    all_to_all x1, starting transfers between devices, on_device(): lax.all_to_all(jnp.stack([query_weight] * lax.axis_size('ctx')), 'ctx', 0...  20.1 us
    unnamed x1, blocking collectives  18.1 us
    add x33, local copies, waits for them, and re-layouts, expand_rows(): values[:, None] + jnp.zeros((1, span_rows), jnp.int32)  12.5 us
  transfers between devices with their start and end apart: 4, of which 3 were waited for; matrix products, arithmetic and copies ran while one was open for 4% of the time, Pallas kernels for 0%

profile of v1, /device:TPU:1, one launch (start us, length us, event | category | flops | bytes accessed | tf_op | source)
XLA Modules:
  0.0 504.0 jit_solution(16308207389114589579)
XLA Ops:
  6.6 0.9 reshape.417
  8.4 0.5 reshape.419
  10.1 0.5 reshape.416
  10.6 1.0 dynamic-slice_convert_fusion
  11.6 1.0 fusion.27
  12.7 2.6 stack.8
  15.3 20.1 %all-to-all-start = ((bf16[64,96,384]{2,1,0:T(8,128)(2,1)}), bf16[64,96,384]{2,1,0:T(8,128)(2,1)}, u32[]{:S(2)}, u32[]{:S(2)}) async-start(bf16[64,96,384]{2,1,0:T(8,128)(2,1)} %stack.8), calls=%async_computation | async-start | bytes 9437184 | tf_op jit(solution)/shard_map/all_to_all | solution.py:138
  35.4 0.7 all-gather.6.cloned.1.call-update
  36.2 0.6 convert_element_type.58
  36.8 76.2 %all-gather.4.cloned.1.call-done = bf16[256,6144]{1,0:T(8,128)(2,1)} async-done(((bf16[256,768]{1,0:T(8,128)(2,1)}), bf16[256,6144]{1,0:T(8,128)(2,1)}) %all-gather.4.cloned.1.call-update) | async-done | bytes 3145744 | tf_op jit(solution)/shard_map/all_gather | solution.py:106
  113.0 2.7 fusion.22
  115.9 1.8 fusion.24
  117.7 185.3 %all-gather.6.cloned.1.call-done = bf16[6144,256]{1,0:T(8,128)(2,1)} async-done(((bf16[96,256]{1,0:T(8,128)(2,1)}), bf16[6144,256]{1,0:T(8,128)(2,1)}) %all-gather.6.cloned.1.call-update) | async-done | bytes 3145744 | tf_op jit(solution)/shard_map/all_gather | solution.py:145
  303.1 3.2 convolution_convert_fusion
  306.3 0.7 fusion.50
  307.1 1.3 dynamic-slice
  309.1 0.5 jit_remainder_.8.clone.1
  309.6 1.1 dynamic-update-slice.1
  311.0 18.1 %all-reduce.4 = (s32[128]{0:T(128)S(1)}, s32[128]{0:T(128)S(1)}) all-reduce(s32[128]{0:T(128)S(1)} %dynamic-update-slice, s32[128]{0:T(128)} %dynamic-update-slice.1), channel_id=1, replica_groups=mesh['ctx'=64,'head'=8] {'ctx'}, use_global_device_ids=true, to_apply=%add.2 | all-reduce | flops 256 | bytes 2048
  329.0 0.7 reshape.426
  329.7 0.7 reshape.427
  330.4 0.5 copy-done.6
  331.0 117.8 %all-gather.8.cloned.1.call-done = bf16[8192,256]{0,1:T(8,128)(2,1)} async-done(((bf16[128,256]{0,1:T(8,128)(2,1)}), bf16[8192,256]{0,1:T(8,128)(2,1)}) %all-gather.8.cloned.1.call-update) | async-done | bytes 4194320 | tf_op jit(solution)/shard_map/all_gather | solution.py:152
  448.8 4.9 copy.132
  453.7 4.0 fusion.31
  457.7 1.0 copy.88
  458.7 1.0 fusion.51
  459.8 0.9 fusion.30
  460.9 35.8 %while.17 = (s32[]{:T(128)}, f32[128,1,3]{0,2,1:T(4,128)S(1)}, f32[128,1,3]{0,2,1:T(4,128)S(1)}, f32[128,1,3,128]{0,3,2,1:T(8,128)S(1)}, s32[8,16]{1,0:T(8,128)}...) while((s32[]{:T(128)}, f32[128,1,3]{0,2,1:T(4,128)S(1)}, ...), condition=%wide.region_6.7_spmd.clone, body=%wide.region_3.6_spmd.clone.sunk | while | flops 205249664 | bytes 7370237 | solution.py:169
  460.9 1.1 constant_dynamic-slice_fusion.4
  462.0 0.7 add.239
  462.8 0.7 fusion.65
  464.1 0.4 fusion.67
  464.9 0.4 fusion.70
  465.4 1.1 constant_dynamic-slice_fusion.4
  466.4 0.7 add.239
  467.3 0.7 fusion.65
  468.6 0.4 fusion.67
  469.4 0.4 fusion.70
  469.8 1.1 constant_dynamic-slice_fusion.4
  470.9 0.7 add.239
  471.7 0.7 fusion.65
  473.1 0.4 fusion.67
  474.3 1.1 constant_dynamic-slice_fusion.4
  475.4 0.7 add.239
  476.2 0.7 fusion.65
  477.6 0.4 fusion.67
  478.8 1.1 constant_dynamic-slice_fusion.4
  479.9 0.7 add.239
  480.7 0.7 fusion.65
  482.0 0.4 fusion.67
  483.3 1.1 constant_dynamic-slice_fusion.4
  484.4 0.7 add.239
  485.2 0.7 fusion.65
  486.5 0.4 fusion.67
  487.8 1.1 constant_dynamic-slice_fusion.4
  488.8 0.7 add.239
  489.7 0.7 fusion.65
  491.0 0.4 fusion.67
  492.2 1.1 constant_dynamic-slice_fusion.4
  493.3 0.7 add.239
  494.1 0.7 fusion.65
  495.5 0.4 fusion.67
  496.8 0.8 copy.94
  (176 shorter events, 14.1 us)
Async XLA Ops:
  6.5 5.1 %copy-start = (bf16[256,768]{1,0:T(8,128)(2,1)S(1)}, bf16[256,768]{1,0:T(8,128)(2,1)}, u32[]{:S(2)}) copy-start(bf16[256,768]{1,0:T(8,128)(2,1)} %param.17) | copy-start | bytes 1179652
  6.5 2.4 copy-start.3
  6.5 2.4 copy-start.8
  6.5 2.4 copy-start.4
  6.5 106.5 %all-gather.4.cloned.1.call-start = ((), (), s32[]{:S(2)}) async-start(), calls=%async_computation.1 | async-start | bytes 3538944 | tf_op jit(solution)/shard_map/all_gather | solution.py:106
  9.5 3.2 copy-start.2
  15.3 20.9 %copy-start.5 = (bf16[6144]{0:T(1024)(128)(2,1)S(1)}, bf16[6144]{0:T(1024)(128)(2,1)}, u32[]{:S(2)}) copy-start(bf16[6144]{0:T(1024)(128)(2,1)} %param.19) | copy-start | bytes 36868
  15.3 438.4 %all-to-all-start = ((bf16[64,96,384]{2,1,0:T(8,128)(2,1)}), bf16[64,96,384]{2,1,0:T(8,128)(2,1)}, u32[]{:S(2)}, u32[]{:S(2)}) async-start(bf16[64,96,384]{2,1,0:T(8,128)(2,1)} %stack.8), calls=%async_computation | async-start | bytes 9437184 | tf_op jit(solution)/shard_map/all_to_all | solution.py:138
  35.4 267.7 %all-gather.6.cloned.1.call-start = ((), (), s32[]{:S(2)}) async-start(), calls=%async_computation.2 | async-start | bytes 3194880 | tf_op jit(solution)/shard_map/all_gather | solution.py:145
  36.1 412.7 %all-gather.8.cloned.1.call-start = ((), (), s32[]{:S(2)}) async-start(), calls=%async_computation.3 | async-start | bytes 4259840 | tf_op jit(solution)/shard_map/all_gather | solution.py:152
  113.0 2.8 copy-start.1
  117.7 189.3 %copy-start.9 = (s32[2]{0:T(128)S(1)}, s32[2]{0:T(128)}, u32[]{:S(2)}) copy-start(s32[2]{0:T(128)} %param.16) | copy-start | bytes 28
  117.7 193.1 %copy-start.10 = (s32[2]{0:T(128)S(1)}, s32[2]{0:T(128)}, u32[]{:S(2)}) copy-start(s32[2]{0:T(128)} %param.15) | copy-start | bytes 28
  330.4 0.5 copy-start.6
  460.9 35.9 %copy-start.7 = (pred[128]{0:T(512)(128)(4,1)S(1)}, pred[128]{0:T(512)(128)(4,1)}, u32[]{:S(2)}) copy-start(pred[128]{0:T(512)(128)(4,1)} %copy-done.6) | copy-start | bytes 388
Sparse Core Ops, SparseCore 0:
  12.8 100.1 all-gather.3
  116.3 186.7 all-gather.5
  307.1 141.6 all-gather.7
